TPU v7x, 256 devices: a whole 4x4x8 slice. The times are simulated.
256 devices in a mesh: state: 64 (over x, y, z_lo), horizon: 4 (over z_hi, core).
Axes of the slice: x: 4, y: 4, z: 8 (z_hi: 2, z_lo: 4; z = z_hi * 4 + z_lo), core: 2. Of those that a mesh axis runs over, the one named last changes fastest.
Arguments:
- expect: bfloat16 [512, 2097152], P('horizon', 'state'), may hold values from -0.00018310547 to 0.00018310547
- steady_dist: float32 [2097152], P('state'), may hold values from 0.2 to 2
- policy_deriv: bfloat16 [128, 2097152], P('horizon', 'state'), may hold values from -16 to 16
- lottery_index: int32 [1024, 2048], P('state'), may hold values from 0 to 2046, as said below
- type_trans: float32 [16, 16], replicated, may hold values from 0.1 to 1
- migration: bfloat16 [64, 2, 16], P('state'), may hold values from 0.049804688 to 0.29882812
- discount: float32 [512], P('horizon'), may hold values from 0.3 to 1
Outputs:
- jacobian: float32 [128, 512], P('state', 'horizon')
- present_value: float32 [128, 512], P('state', 'horizon')
Inputs may be any that keep to these rules, and one draw needn't show every extreme that they name: `lottery_index`: for every row and every block of 128 asset nodes, every index of the block lies between 128 * (m // 128) and 128 * (m // 128) + 254, where m is the block's smallest index.
All inputs are finite; a program needn't handle non-finite values.
Results may differ from a plain program's by a relative error of at most 0.0072.
Values may be sent and summed in bfloat16 or wider, within the bound.
A program may use at most 128 MiB of HBM per device.

v0:
```python
import jax
import jax.numpy as jnp
from jax import lax
from jax.sharding import PartitionSpec as P


def carried_in(value, axis, join, neutral):
    count, mine = (lax.axis_size(axis), lax.axis_index(axis))
    pieces = jax.tree.map(lambda part: lax.all_gather(part, axis), value)
    pieces = jax.tree.map(lambda part: part[::-1], pieces)
    mine = count - 1 - mine
    running = jax.tree.map(
        lambda part, zero: jnp.full_like(part, 0) + jnp.asarray(zero, part.dtype), value, neutral
    )

    def hop(position, running):
        longer = join(running, jax.tree.map(lambda part: part[position], pieces))
        return jax.tree.map(lambda new, old: jnp.where(position < mine, new, old), longer, running)

    return lax.fori_loop(0, count - 1, hop, running)


def shifted(block, axis, distance):
    devices = range(lax.axis_size(axis))
    route = [((i - distance) % len(devices), i) for i in devices]
    return lax.ppermute(block, axis, route)


def shifted_2(value, axis, by):
    peers = lax.axis_size(axis)
    pairs = [(i, i + by) for i in range(peers) if 0 <= i + by < peers]
    return lax.ppermute(value, axis, pairs)


def weigh(entering_lines, switching_intensities):
    height = entering_lines.shape[0]
    scaled = (
        entering_lines.astype(jnp.float32).reshape(height, switching_intensities.shape[0], -1)
        * switching_intensities[None, :, None]
    )
    return scaled.reshape(height, -1).astype(jnp.bfloat16)


def against(left_rows, right_rows):
    return lax.dot_general(
        left_rows, right_rows, (((1,), (1,)), ((), ())), preferred_element_type=jnp.float32
    )


def build_shift(policy_deriv, steady_dist, lottery_index, type_trans):
    num_cols = policy_deriv.shape[0]
    num_states = policy_deriv.shape[1]
    household_type_count = lottery_index.shape[0]
    num_assets = lottery_index.shape[1]
    blocks = num_assets // 128
    masses = (steady_dist[None, :] * policy_deriv.astype(jnp.float32)).astype(jnp.bfloat16)
    masses = masses.reshape(num_cols, household_type_count, blocks, 128)
    node_ids = lottery_index.reshape(household_type_count, blocks, 128)
    starts = jnp.min(node_ids, axis=2) // 128
    offsets = (node_ids - 128 * starts[:, :, None])[..., None]
    target = lax.broadcasted_iota(jnp.int32, (1, 1, 1, 256), 3)
    lottery = jnp.where(target == offsets, 1.0, jnp.where(target == offsets + 1, -1.0, 0.0)).astype(
        jnp.bfloat16
    )
    dispersion_width = jnp.einsum(
        "cxki,xkij->cxkj", masses, lottery, preferred_element_type=jnp.float32
    )
    dispersion_width = dispersion_width.reshape(num_cols, household_type_count, blocks, 2, 128)
    block_ids = lax.broadcasted_iota(jnp.int32, (1, 1, 2, blocks), 3)
    halves = lax.broadcasted_iota(jnp.int32, (1, 1, 2, blocks), 2)
    placing = (block_ids == starts[:, :, None, None] + halves).astype(jnp.float32)
    landed = jnp.einsum(
        "cxkhi,xkhb->cxbi", dispersion_width, placing, precision=lax.Precision.HIGHEST
    )
    type_mix = type_trans / jnp.sum(type_trans, axis=1, keepdims=True)
    blended = jnp.einsum("cxbi,xy->cybi", landed, type_mix, precision=lax.Precision.HIGHEST)
    return blended.reshape(num_cols, num_states).astype(jnp.bfloat16)


def diagonal_sum(current, previous):
    num_cols = current.shape[0]
    height = current.shape[1]
    stacked = jnp.concatenate([previous, current], axis=1)
    offset = 1
    while offset < num_cols:
        lagged = jnp.pad(stacked, ((offset, 0), (offset, 0)))[:num_cols, : 2 * height]
        stacked = stacked + lagged
        offset = offset * 2
    return stacked[:, height:]


def discounted(jac_rows, discount):
    height = discount.shape[0]
    log_rates = jnp.log(discount)
    before = jnp.cumsum(log_rates) - log_rates
    later_ids = lax.broadcasted_iota(jnp.int32, (height, height), 0)
    column_ids = lax.broadcasted_iota(jnp.int32, (height, height), 1)
    patience_betas = jnp.where(
        later_ids >= column_ids, jnp.exp(before[:, None] - before[None, :]), 0.0
    )
    local_value = jnp.dot(jac_rows, patience_betas, precision=lax.Precision.HIGHEST)
    log_total = jnp.sum(log_rates)
    remaining = jnp.exp(log_total - before)

    def combine(earlier, later):
        return (later[0] * earlier[0], later[1] + later[0] * earlier[1])

    _, incoming = carried_in(
        (jnp.exp(log_total)[None], local_value[:, 0]),
        "horizon",
        combine,
        (jnp.ones((1,), jnp.float32), jnp.zeros_like(local_value[:, 0])),
    )
    return local_value + remaining[None, :] * incoming[:, None]


def local(expect, steady_dist, policy_deriv, lottery_index, type_trans, migration, discount):
    own_rates = migration[0].astype(jnp.float32)
    stay_rates = 1.0 - own_rates[0] - own_rates[1]
    home_rows = weigh(expect, stay_rates)
    own_shift = build_shift(policy_deriv, steady_dist, lottery_index, type_trans)
    all_shift = lax.all_gather(own_shift, "horizon", axis=0, tiled=True)
    shift_below, rates_below = shifted((all_shift, migration), "state", 1)
    shift_above, rates_above = shifted((all_shift, migration), "state", -1)
    flow_part = against(all_shift, home_rows)
    flow_part = flow_part + against(
        shift_below, weigh(expect, rates_below[0, 1].astype(jnp.float32))
    )
    flow_part = flow_part + against(
        shift_above, weigh(expect, rates_above[0, 0].astype(jnp.float32))
    )
    flow_total = lax.psum(flow_part, "state")
    flow_before = shifted_2(flow_total, "horizon", 1)
    jac_all = diagonal_sum(flow_total, flow_before)
    col_share = jac_all.shape[0] // lax.axis_size("state")
    jac_rows = lax.dynamic_slice_in_dim(jac_all, lax.axis_index("state") * col_share, col_share, 0)
    return (jac_rows, discounted(jac_rows, discount))


def solution(mesh):
    return jax.shard_map(
        local,
        mesh=mesh,
        in_specs=(
            P("horizon", "state"),
            P("state"),
            P("horizon", "state"),
            P("state", None),
            P(),
            P("state", None, None),
            P("horizon"),
        ),
        out_specs=(P("state", "horizon"), P("state", "horizon")),
        check_vma=False,
    )
```

profile of v0, /device:TPU:1, one launch (start us, length us, event | category | flops | bytes accessed | tf_op | source)
XLA Modules:
  0.0 1221.4 jit_solution(8879146471718469078)
XLA Ops:
  7.2 0.0 all-gather.3.cloned.1.call-start
  7.2 0.9 copy.21
  8.1 0.3 reduce_min.9
  8.5 0.1 broadcast_add_fusion
  8.6 2.0 fusion.24
  10.6 0.5 copy.22
  11.1 16.5 %fusion.23 = f32[32,16,16,256]{3,0,2,1:T(8,128)} fusion(s32[16,16,128]{2,1,0:T(8,128)S(1)} %get-tuple-element.129, s32[16,16,128]{2,1,0:T(8,128)S(1)} %get-tuple-element.130, bf16[32,16,16,128]{3,2,1,0:T(8,128)(2,1)S(1)} %bitcast.72), kind=kOutput, calls=%fused_computation.31 | convolution fusion | flops 578813952 | bytes 10747904 | tf_op jit(solution)/shard_map/cxki,xkij->cxkj/dot_general | solution.py:65
  27.6 10.8 reshape.139
  38.4 0.3 compare_bitcast_fusion
  38.7 12.1 fusion.15
  50.9 0.1 reduce_sum.18
  51.0 8.2 convert_bitcast_fusion
  59.2 0.5 copy.14
  59.7 2.7 copy.41
  62.4 0.0 all-gather.3.cloned.1.call-update
  62.4 0.0 all-reduce.12.cloned.1.call-start
  62.5 117.9 %all-gather.3.cloned.1.call-done = bf16[128,32768]{1,0:T(8,128)(2,1)} async-done(((bf16[32,32768]{1,0:T(8,128)(2,1)}), bf16[128,32768]{1,0:T(8,128)(2,1)}) %all-gather.3.cloned.1.call-update) | async-done | bytes 8388624 | tf_op jit(solution)/shard_map/all_gather | solution.py:122
  180.4 1.5 collective-permute-start
  181.8 6.0 collective-permute-start.3
  187.9 0.1 broadcast_bitcast_fusion.2
  188.0 354.3 %collective-permute-done.3 = bf16[1,2,16]{2,1,0:T(2,128)(2,1)S(1)} collective-permute-done((bf16[1,2,16]{2,1,0:T(2,128)(2,1)S(1)}, bf16[1,2,16]{2,1,0:T(2,128)(2,1)S(1)}, u32[]{:S(2)}, u32[]{:S(2)}) %collective-permute-start.3) | collective-permute-done | bytes 96 | tf_op jit(solution)/shard_map/ppermute | solution.py:26
  542.3 0.1 broadcast_bitcast_fusion
  542.4 3.0 collective-permute-done.1
  545.4 0.1 broadcast_bitcast_fusion.1
  545.5 0.0 slice-start
  545.5 8.3 fusion.13
  553.8 0.0 slice-start.1
  553.8 8.3 fusion.9
  562.1 3.2 copy-done.3
  565.4 0.0 copy-start.5
  565.4 6.7 fusion.31
  572.0 0.0 all-reduce.12.cloned.1.call-update
  572.1 0.6 log_bitcast_fusion
  572.7 0.1 copy.15
  572.8 0.2 reduce-window.9
  572.9 0.1 reduce
  573.1 598.8 %all-reduce.12.cloned.1.call-done = f32[128,128]{1,0:T(8,128)} async-done(((f32[128,128]{1,0:T(8,128)}), f32[128,128]{1,0:T(8,128)}) %all-reduce.12.cloned.1.call-update) | async-done | bytes 65552 | tf_op jit(solution)/shard_map/psum | solution.py:132
  1171.8 23.6 %collective-permute-start.4 = (f32[128,128]{1,0:T(8,128)}, f32[128,128]{1,0:T(8,128)S(1)}, u32[]{:S(2)}, u32[]{:S(2)}) collective-permute-start(f32[128,128]{1,0:T(8,128)} %all-reduce.12.cloned.1.call-done), channel_id=1, source_target_pairs={{0,1},{1,2},{2,3},{4,5},{5,6},{6,7},{8,9},{9,10},{10,11},{12,13},{... | collective-permute-start | bytes 196616 | tf_op jit(solution)/shard_map/ppermute | solution.py:32
  1195.4 0.7 subtract_exponential_fusion
  1196.8 0.6 dynamic-slice
  1198.0 0.8 dynamic-update-slice.1
  1198.8 0.8 constant_dynamic-update-slice_fusion
  1199.6 0.1 fusion.35
  1199.7 0.1 fusion.36
  1199.8 0.1 fusion.37
  1200.0 0.1 fusion.38
  1200.1 0.1 fusion.39
  1200.2 0.1 fusion.40
  1200.3 0.1 pad_slice_fusion
  1200.4 0.0 copy-start.1
  1200.4 0.2 fusion.41
  1200.6 0.1 slice_reduce_fusion
  1200.8 0.2 dynamic-update-slice
  1201.0 9.0 all-reduce.9
  1210.0 0.1 reshape.144
  1210.1 0.1 reverse
  1210.2 3.7 while.14
  1210.2 0.6 constant_dynamic-slice_fusion.2
  1210.8 0.6 broadcast_select_fusion.3
  1211.5 0.6 constant_dynamic-slice_fusion.2
  1212.1 0.6 broadcast_select_fusion.3
  1212.7 0.6 constant_dynamic-slice_fusion.2
  1213.3 0.6 broadcast_select_fusion.3
  1214.0 0.6 multiply_add_fusion
  (33 shorter events, 0.2 us)
Async XLA Ops:
  7.2 173.2 %all-gather.3.cloned.1.call-start = ((), (), s32[]{:S(2)}) async-start(), calls=%async_computation | async-start | bytes 10485760 | tf_op jit(solution)/shard_map/all_gather | solution.py:122
  38.4 12.5 %copy-start = (f32[16,16]{1,0:T(8,128)S(1)}, f32[16,16]{1,0:T(8,128)}, u32[]{:S(2)}) copy-start(f32[16,16]{1,0:T(8,128)} %param.13) | copy-start | bytes 3076
  51.0 130.8 %copy-start.4 = (bf16[1,2,16]{2,1,0:T(2,128)(2,1)S(1)}, bf16[1,2,16]{2,1,0:T(2,128)(2,1)}, u32[]{:S(2)}) copy-start(bf16[1,2,16]{2,1,0:T(2,128)(2,1)} %param.14) | copy-start | bytes 196
  62.4 1109.4 %all-reduce.12.cloned.1.call-start = ((), (), s32[]{:S(2)}) async-start(), calls=%async_computation.1 | async-start | bytes 131072 | tf_op jit(solution)/shard_map/psum | solution.py:132
  180.4 373.4 %collective-permute-start.2 = (bf16[128,32768]{1,0:T(8,128)(2,1)}, bf16[128,32768]{1,0:T(8,128)(2,1)}, u32[]{:S(2)}, u32[]{:S(2)}) collective-permute-start(bf16[128,32768]{1,0:T(8,128)(2,1)} %all-gather.3.cloned.1.call-done), channel_id=1, source_target_pairs={{4,0},{8,4},{12,8},{16,12},{20,16},{24,20},{28,24},{32,28},{36,32}... | collective-permute-start | bytes 25165832 | tf_op jit(solution)/shard_map/ppermute | solution.py:26
  180.4 381.8 %collective-permute-start = (bf16[128,32768]{1,0:T(8,128)(2,1)}, bf16[128,32768]{1,0:T(8,128)(2,1)S(1)}, u32[]{:S(2)}, u32[]{:S(2)}) collective-permute-start(bf16[128,32768]{1,0:T(8,128)(2,1)} %all-gather.3.cloned.1.call-done), channel_id=1, source_target_pairs={{252,0},{0,4},{4,8},{8,12},{12,16},{16,20},{20,24},{24,28},{28,32}... | collective-permute-start | bytes 25165832 | tf_op jit(solution)/shard_map/ppermute | solution.py:26
  181.8 360.4 %collective-permute-start.3 = (bf16[1,2,16]{2,1,0:T(2,128)(2,1)S(1)}, bf16[1,2,16]{2,1,0:T(2,128)(2,1)S(1)}, u32[]{:S(2)}, u32[]{:S(2)}) collective-permute-start(bf16[1,2,16]{2,1,0:T(2,128)(2,1)S(1)} %copy-done.4), channel_id=1, source_target_pairs={{4,0},{8,4},{12,8},{16,12},{20,16},{24,20},{28,24},{32,28},{36,32}... | collective-permute-start | bytes 200 | tf_op jit(solution)/shard_map/ppermute | solution.py:26
  187.8 357.5 %collective-permute-start.1 = (bf16[1,2,16]{2,1,0:T(2,128)(2,1)S(1)}, bf16[1,2,16]{2,1,0:T(2,128)(2,1)S(1)}, u32[]{:S(2)}, u32[]{:S(2)}) collective-permute-start(bf16[1,2,16]{2,1,0:T(2,128)(2,1)S(1)} %copy-done.4), channel_id=1, source_target_pairs={{252,0},{0,4},{4,8},{8,12},{12,16},{16,20},{20,24},{24,28},{28,32}... | collective-permute-start | bytes 200 | tf_op jit(solution)/shard_map/ppermute | solution.py:26
  545.5 19.9 %slice-start = ((s8[8388608]{0:T(1024)(128)(4,1)}), s8[4194304]{0:T(1024)(128)(4,1)S(1)}, s32[]{:S(2)}) async-start(s8[8388608]{0:T(1024)(128)(4,1)} %bitcast.78), calls=%async_computation.2 | async-start | bytes 8388608
  553.8 11.5 slice-start.1
  562.1 3.2 copy-start.3
  565.4 6.7 copy-start.2
  565.4 631.4 %copy-start.5 = (u32[256]{0:T(256)S(1)}, u32[256]{0:T(256)}, u32[]{:S(2)}) copy-start(u32[256]{0:T(256)} %constant.87) | copy-start | bytes 3076
  1171.8 26.9 %collective-permute-start.4 = (f32[128,128]{1,0:T(8,128)}, f32[128,128]{1,0:T(8,128)S(1)}, u32[]{:S(2)}, u32[]{:S(2)}) collective-permute-start(f32[128,128]{1,0:T(8,128)} %all-reduce.12.cloned.1.call-done), channel_id=1, source_target_pairs={{0,1},{1,2},{2,3},{4,5},{5,6},{6,7},{8,9},{9,10},{10,11},{12,13},{... | collective-permute-start | bytes 196616 | tf_op jit(solution)/shard_map/ppermute | solution.py:32
  1200.4 14.2 %copy-start.1 = (f32[2,128]{1,0:T(2,128)}, f32[2,128]{1,0:T(2,128)S(1)}, u32[]{:S(2)}) copy-start(f32[2,128]{1,0:T(2,128)S(1)} %dynamic-slice_add_fusion) | copy-start | bytes 3076
Sparse Core Ops, SparseCore 0:
  62.6 117.7 all-gather.2
  572.2 599.6 all-reduce.11
where the time goes:
time: 1220 us
  waiting for transfers between devices  1070 us (88%)
  matrix products  60.2 us (5%)
  starting transfers between devices  31.1 us (3%)
  local copies, waits for them, and re-layouts  23.8 us (2%)
  between operations  15.7 us (1%)
    psum x1, waiting for transfers between devices, local(): flow_total = lax.psum(flow_part, 'state')  599 us
    ppermute x4, waiting for transfers between devices, shifted(): return lax.ppermute(block, axis, route)  357 us
    all_gather x1, waiting for transfers between devices, local(): all_shift = lax.all_gather(own_shift, 'horizon', axis=0, tiled=True)  118 us
  transfers between devices with their start and end apart: 7, of which 4 were waited for; matrix products, arithmetic and copies ran while one was open for 2% of the time, Pallas kernels for 0%

commit v1 on v0

v1 whole, which is shorter than its diff:
```python
import jax
import jax.numpy as jnp
from jax import lax
from jax.experimental import pallas as pl
from jax.experimental.pallas import tpu as pltpu
from jax.sharding import PartitionSpec as P

MESH = pl.DeviceIdType.MESH
BLOCK = 128
CHUNKS = 8
PARTS = 4
STEPS = 5
ONE_HOP = STEPS + 1
NT = (((1,), (1,)), ((), ()))
bf = jnp.bfloat16
f32 = jnp.float32


def locate(index, offsets, keys):
    types = index.shape[0]
    blocks = offsets.shape[0]
    lane = lax.broadcasted_iota(jnp.int32, (types, 4*BLOCK), 1)
    acc = lane // (16*blocks) + 16 * (lane % 16)
    acc = acc.astype(f32)
    for k in range(blocks):
        nodes = index[:, k*BLOCK:(k+1)*BLOCK]
        base = lax.shift_right_logical(jnp.min(nodes, axis=1, keepdims=True), 7)
        away = (nodes - base * BLOCK).astype(f32)
        offsets[k] = away
        acc = acc + jnp.where((lane // 16) % blocks == k, base.astype(f32), 0.0)
    for q in range(4):
        keys[q] = acc[:, q*BLOCK:(q+1)*BLOCK]


def spread_mix(trans, kron):
    types = trans.shape[0]
    mix = trans[...] / jnp.sum(trans[...], axis=1, keepdims=True)
    high = mix.astype(bf)
    low = (mix - high.astype(f32)).astype(bf)
    wide = types*16
    tall = lax.broadcasted_iota(jnp.int32,(wide,types),0)//16 == lax.broadcasted_iota(jnp.int32,(wide,types),1)
    tall = jnp.where(tall,1.0,0.0).astype(bf)
    same = lax.broadcasted_iota(jnp.int32,(wide,wide),0)%16 == lax.broadcasted_iota(jnp.int32,(wide,wide),1)%16
    for n, part in enumerate((high, low)):
        left = lax.dot_general(tall, part, NT, preferred_element_type=f32)
        both = lax.dot_general(left.astype(bf), tall, NT, preferred_element_type=f32)
        kron[n*wide:(n+1)*wide, :] = jnp.where(same, both, 0.0).astype(bf)

def land_pieces(mass, offsets, keys, kron, moved, landed, out):
    types = keys.shape[1]
    blocks = offsets.shape[0]
    cols = mass.shape[0]
    assets = blocks * BLOCK
    wide = types * 16
    node = lax.broadcasted_iota(jnp.int32, (2 * BLOCK, BLOCK), 0).astype(f32).astype(bf)

    def halves(value):
        high = value.astype(bf)
        return high, (value - high.astype(f32)).astype(bf)

    def one_block(k):
        for x in range(types):
            lanes = pl.ds(pl.multiple_of(x * assets + k * BLOCK, BLOCK), BLOCK)
            away = offsets[k, x : x + 1, :]
            here, there = away.astype(bf), (away + 1.0).astype(bf)
            lottery = jnp.where(node == here, bf(1), jnp.where(node == there, bf(-1), bf(0)))
            got = lax.dot_general(mass[:, lanes], lottery, NT, preferred_element_type=f32)
            for n, part in enumerate(halves(got)):
                for h in range(2):
                    rows = pl.ds(pl.multiple_of(h * blocks * 16 + k * 16, 16), 16)
                    for g in range(cols // 16):
                        moved[n, x, rows, g * BLOCK : (g + 1) * BLOCK] = part[
                            g * 16 : (g + 1) * 16, h * BLOCK : (h + 1) * BLOCK
                        ]

    row = lax.broadcasted_iota(jnp.int32, (blocks * 16, 4 * BLOCK), 0)
    row_key = (row // 16 + 16 * (row % 16)).astype(f32).astype(bf)

    def one_type(x):
        key = jnp.concatenate([keys[q, pl.ds(x, 1), :] for q in range(4)], axis=1)
        place = jnp.where(row_key == key.astype(bf), bf(1), bf(0))
        total = jnp.dot(place, moved[0, x], preferred_element_type=f32)
        total += jnp.dot(place, moved[1, x], preferred_element_type=f32)
        rows = pl.ds(pl.multiple_of(x * 16, 16), 16)
        for n, part in enumerate(halves(total)):
            for b in range(blocks):
                for g in range(cols // 16):
                    landed[n, g, rows, b * BLOCK : (b + 1) * BLOCK] = part[
                        b * 16 : (b + 1) * 16, g * BLOCK : (g + 1) * BLOCK
                    ]

    tile = 256

    def blend(n):
        lanes = pl.ds(pl.multiple_of(n * tile, tile), tile)
        for g in range(cols // 16):
            both = jnp.dot(kron[...], landed[0, g, :, lanes], preferred_element_type=f32)
            rest = jnp.dot(kron[0:wide, :], landed[1, g, :, lanes], preferred_element_type=f32)
            total = (both[:wide] + both[wide:] + rest).astype(bf)
            for y in range(types):
                out[y * cols + g * 16 : y * cols + g * 16 + 16, lanes] = total[
                    y * 16 : (y + 1) * 16
                ]

    return (blocks, one_block), (types, one_type), (assets // tile, blend)


def flow_kernel(
    expect_in, policy_in, steady_in, index_in, trans_in, migration_in, discount_in, jac_out, value_out,
    lines, held, flow, half, pairs, from_plane, from_line, betas, wide, powers,
    mass, raw, steady, nodes, short, trans, moves, rates, weights, offsets, keys, kron, moved, landed, discount,
    local_sem, send_sem, recv_sem, last_sem, tail_send, tail_recv,
):
    state, horizon = lax.axis_index("state"), lax.axis_index("horizon")
    core, upper, low = horizon % 2, horizon // 2, state % 4
    z = upper * 4 + low
    way = 1 - 2 * core
    rows_all, assets = held.shape[1:]
    types = trans.shape[0]
    cols = rows_all // types
    chunk_rows = rows_all // CHUNKS
    chunk_types = types // CHUNKS
    shifts = {1: 1, 3: -1, 4: 0, 5: 1}

    def origin(step):
        z0 = (z - way * step + 40) % 8
        if step == 0:
            return state, z0
        if step == 2:
            return state - low + z0 % 4, z0
        return (state - way * shifts[step] + 64) % 64, z0

    def place(region, z0, step):
        at = (z0 + way * step + 40) % 8
        if step == 2:
            there = region - region % 4 + at % 4
        else:
            there = (region + way * shifts[step] + 64) % 64
        return there, (at // 4) * 2 + core

    def target(step):
        return place(*origin(step - 1), step)

    def source(step):
        region, z0 = origin(step)
        return place(region, z0, step - 1) if step > 1 else (region, (z0 // 4) * 2 + core)

    hop_to = ((state - way + 64) % 64, ((z - way + 8) % 8 // 4) * 2 + core)
    hop_from = ((state + way + 64) % 64, ((z + way + 8) % 8 // 4) * 2 + core)
    other = (state, horizon + way)
    ahead = ((state + 1) % 64, ((z + 1) % 8 // 4) * 2 + core)
    behind = ((state + 63) % 64, ((z + 7) % 8 // 4) * 2 + core)
    column = state // 4

    def plane_at(dx, dy):
        return ((column // 4 + dx) % 4) * 4 + (column + dy) % 4

    def plane_peer(dx, dy):
        return (plane_at(dx, dy) * 4 + low, horizon)

    def line_peer(dz, flip):
        at = (z + dz) % 8
        return (state - low + at % 4, (at // 4) * 2 + core + flip * way)

    def mate(dh):
        return (state, (horizon + dh) % 4)

    far = (2, 1, 3, 0)
    plane_turns = sorted(
        [(dx, dy) for dx in far for dy in far if dx or dy], key=lambda t: far.index(t[0]) + far.index(t[1])
    )
    line_turns = [(dz, flip) for dz in (4, 3, 5, 2, 6, 1, 7, 0) for flip in (0, 1) if dz or flip]
    span = assets * types // PARTS

    def part(n):
        return pl.ds(n * span, span)

    loads = [
        pltpu.make_async_copy(src, dst, local_sem.at[n])
        for n, (src, dst) in enumerate(
            [
                (steady_in, steady),
                (migration_in, moves),
                (index_in, nodes),
                (discount_in, discount),
                (trans_in, trans),
                (expect_in, lines.at[core]),
            ]
            + [(policy_in.at[:, part(n)], mass.at[:, part(n)]) for n in range(PARTS)]
        )
    ]
    for load in loads[:5] + loads[6:] + loads[5:6]:
        load.start()
    barrier = pltpu.get_barrier_semaphore()
    greeted = [source(step) for step in range(1, STEPS + 1)] + [hop_from, other, ahead, behind]
    greeted += [plane_peer(-dx % 4, -dy % 4) for dx, dy in plane_turns]
    greeted += [line_peer(-dz % 8, flip) for dz, flip in line_turns]
    for peer in greeted:
        pl.semaphore_signal(barrier, inc=1, device_id=peer, device_id_type=MESH)

    for load in loads[:5]:
        load.wait()
    short[0] = nodes[...].astype(jnp.int16)
    rates[0] = jnp.zeros((8, BLOCK), f32)
    rates[0, 0:2, 0:types] = moves[...].astype(f32)
    each = assets // BLOCK

    def weigh(x, carry):
        for n in range(each):
            lanes = pl.ds(pl.multiple_of(x * assets + n * BLOCK, BLOCK), BLOCK)
            factor = steady[pl.ds(x * each + n, 1), :]
            mass[:, lanes] = (factor * mass[:, lanes].astype(f32)).astype(bf)
        return carry

    def chunk(c):
        return pl.ds(pl.multiple_of(c * chunk_rows, chunk_rows), chunk_rows)

    def move(step, c):
        return pltpu.make_async_remote_copy(
            src_ref=held.at[step - 1, chunk(c)],
            dst_ref=held.at[step, chunk(c)],
            send_sem=send_sem.at[step],
            recv_sem=recv_sem.at[step, c],
            device_id=target(step),
            device_id_type=MESH,
        )

    def last_move(y):
        rows = pl.ds(pl.multiple_of(y * cols, cols), cols)
        return pltpu.make_async_remote_copy(
            src_ref=held.at[STEPS - 1, rows],
            dst_ref=held.at[STEPS, rows],
            send_sem=send_sem.at[STEPS],
            recv_sem=last_sem.at[y],
            device_id=target(STEPS),
            device_id_type=MESH,
        )

    def across(src, dst, n, to):
        return pltpu.make_async_remote_copy(
            src_ref=src,
            dst_ref=dst,
            send_sem=tail_send.at[28 + n],
            recv_sem=tail_recv.at[28 + n],
            device_id=to,
            device_id_type=MESH,
        )

    early_moves = [
        across(rates.at[0], rates.at[1], 0, ahead),
        across(short.at[0], short.at[1], 1, hop_to),
        across(rates.at[0], rates.at[2], 2, behind),
        across(expect_in, lines.at[core], 3, other),
    ]
    lines_landed = across(expect_in, lines.at[1 - core], 3, other)
    raw_moves = [
        across(mass.at[:, part(n)], raw.at[:, part(n)], 4 + n, hop_to) for n in range(PARTS)
    ]
    for n in range(PARTS):
        loads[6 + n].wait()
        lax.fori_loop(n * types // PARTS, (n + 1) * types // PARTS, weigh, 0)
        if n == 0:
            pl.semaphore_wait(barrier, len(greeted))
        raw_moves[n].start()
    for copy in early_moves:
        copy.start()

    def beta_move(dh):
        return pltpu.make_async_remote_copy(
            src_ref=discount,
            dst_ref=betas.at[horizon],
            send_sem=tail_send.at[24 + dh],
            recv_sem=tail_recv.at[24 + dh],
            device_id=mate(dh),
            device_id_type=MESH,
        )

    def loop(body):
        lax.fori_loop(0, CHUNKS, lambda c, carry: (body(c), carry)[1], 0)

    for dh in (1, 2, 3):
        beta_move(dh).start()
    betas[horizon] = discount[...]

    spread_mix(trans, kron)
    locate(nodes, offsets, keys)
    for count, piece in land_pieces(mass, offsets, keys, kron, moved, landed, held.at[0]):
        lax.fori_loop(0, count, lambda n, carry, piece=piece: (piece(n), carry)[1], 0)
    loop(lambda c: move(1, c).start())

    early_moves[0].wait_recv()
    early_moves[2].wait_recv()
    diagonal = lax.broadcasted_iota(jnp.int32, (types, BLOCK), 0) == lax.broadcasted_iota(
        jnp.int32, (types, BLOCK), 1
    )
    mine = 1.0 - rates[0, 0:1, :] - rates[0, 1:2, :]
    for n, line in enumerate((mine, rates[1, 1:2, :], rates[2, 0:1, :])):
        upright = jnp.sum(jnp.where(diagonal, line, 0.0), axis=1, keepdims=True)
        weights[n] = jnp.broadcast_to(upright, (types, BLOCK))

    for copy in raw_moves:
        copy.wait_recv()
    early_moves[1].wait_recv()
    nodes[...] = short[1].astype(jnp.int32)
    locate(nodes, offsets, keys)
    pieces = land_pieces(raw, offsets, keys, kron, moved, landed, held.at[ONE_HOP])

    for step in range(1, STEPS - 1):

        def onward(c, step=step):
            move(step, c).wait_recv()
            move(step + 1, c).start()
            count, piece = pieces[step - 1]
            for n in range(count // CHUNKS):
                piece(c * (count // CHUNKS) + n)

        loop(onward)

    mirror = low + core * (3 - 2 * low)
    edge_low, edge_high = (3 - mirror) // 3, mirror // 3
    edge = edge_low + edge_high

    def multiply(late, y):
        same = 4 * (1 - edge_low) if late else 4 * edge_low
        prior = STEPS if late else 1
        after = 3 + 3 * edge if late else 6 - 3 * edge
        rows = pl.ds(pl.multiple_of(y * cols, cols), cols)
        total = None
        for n, slot in ((0, same), (1 + core, prior), (2 - core, after)):
            weight = jnp.concatenate([weights[n, pl.ds(y, 1), :]] * (assets // BLOCK), axis=1)
            term = held[slot, rows, :].astype(f32) * weight
            total = term if total is None else total + term
        lanes = pl.ds(pl.multiple_of(y * assets, assets), assets)
        right = jnp.concatenate([lines[0, :, lanes], lines[1, :, lanes]], axis=0)
        high = total.astype(bf)
        left = jnp.concatenate([high, (total - high.astype(f32)).astype(bf)], axis=0)
        both = lax.dot_general(left, right, NT, preferred_element_type=f32)
        flow[late] += both[:cols] + both[cols:]

    def beta_landed(dh):
        return pltpu.make_async_remote_copy(
            src_ref=discount,
            dst_ref=betas.at[(horizon + 4 - dh) % 4],
            send_sem=tail_send.at[24 + dh],
            recv_sem=tail_recv.at[24 + dh],
            device_id=mate(dh),
            device_id_type=MESH,
        )

    for dh in (1, 2, 3):
        beta_landed(dh).wait_recv()
    length = 4 * BLOCK
    hops = length.bit_length() - 1
    ids = lax.broadcasted_iota(jnp.int32, (2, length), 1)
    factor = jnp.concatenate([betas[h] for h in range(4)], axis=1)
    factor = jnp.broadcast_to(factor, (2, length))
    for n in range(hops):
        powers[n] = factor
        lagged = pltpu.roll(factor, length - 2**n, 1)
        factor = factor * jnp.where(ids < length - 2**n, lagged, 0.0)

    loads[5].wait()
    lines_landed.wait_recv()
    flow[...] = jnp.zeros_like(flow)

    def early(c):
        move(STEPS - 1, c).wait_recv()
        for i in range(chunk_types):
            last_move(c * chunk_types + i).start()
        for i in range(chunk_types):
            multiply(0, c * chunk_types + i)

    loop(early)

    def late(y, carry):
        last_move(y).wait_recv()
        multiply(1, y)
        return carry

    lax.fori_loop(0, types, late, 0)

    late_half = upper + (1 - edge_low) * (1 - 2 * upper)
    half[...] = jnp.zeros_like(half)
    for when, at in ((0, 1 - late_half), (1, late_half)):
        rows = pl.ds(pl.multiple_of((at * 2 + core) * cols, cols), cols)
        half[rows, : 2 * BLOCK] = flow[when]
    total = half[...]
    rows_at = lax.broadcasted_iota(jnp.int32, total.shape, 0)
    offset = 1
    while offset < 4 * cols:
        lagged = pltpu.roll(pltpu.roll(total, offset, 0), offset, 1)
        total = total + jnp.where(rows_at >= offset, lagged, 0.0)
        offset *= 2
    half[...] = total

    def plane_move(n, dx, dy):
        block = pl.ds(pl.multiple_of(plane_at(dx, dy) * 8, 8), 8)
        return pltpu.make_async_remote_copy(
            src_ref=half.at[block],
            dst_ref=from_plane.at[n],
            send_sem=tail_send.at[0],
            recv_sem=tail_recv.at[0],
            device_id=plane_peer(dx, dy),
            device_id_type=MESH,
        )

    def plane_all():
        return pltpu.make_async_remote_copy(
            src_ref=half.at[pl.ds(0, 8 * len(plane_turns))],
            dst_ref=from_plane,
            send_sem=tail_send.at[0],
            recv_sem=tail_recv.at[0],
            device_id=plane_peer(1, 0),
            device_id_type=MESH,
        )

    for n, (dx, dy) in enumerate(plane_turns):
        plane_move(n, dx, dy).start()

    for step in range(1, STEPS + 1):
        pltpu.make_async_remote_copy(
            src_ref=held.at[step - 1],
            dst_ref=held.at[step],
            send_sem=send_sem.at[step],
            recv_sem=recv_sem.at[1, 0],
            device_id=target(step),
            device_id_type=MESH,
        ).wait_send()
    for copy in early_moves + raw_moves:
        copy.wait_send()
    for k in (1, 2, 3):
        beta_move(k).wait_send()

    plane_all().wait_recv()
    parts = [half[pl.ds(pl.multiple_of(column * 8, 8), 8), :]]
    parts += [from_plane[n] for n in range(15)]
    while len(parts) > 1:
        parts = [a + b for a, b in zip(parts[::2], parts[1::2])]
    for q in range(4):
        pairs[q] = parts[0][2 * q : 2 * q + 2]
    here = z * 2 + core

    def line_move(dz, flip):
        return pltpu.make_async_remote_copy(
            src_ref=pairs.at[(low + dz) % 4],
            dst_ref=from_line.at[here],
            send_sem=tail_send.at[1],
            recv_sem=tail_recv.at[1],
            device_id=line_peer(dz, flip),
            device_id_type=MESH,
        )

    def line_all():
        return pltpu.make_async_remote_copy(
            src_ref=from_line.at[pl.ds(0, len(line_turns))],
            dst_ref=from_line.at[pl.ds(0, len(line_turns))],
            send_sem=tail_send.at[1],
            recv_sem=tail_recv.at[1],
            device_id=line_peer(1, 0),
            device_id_type=MESH,
        )

    for dz, flip in line_turns:
        line_move(dz, flip).start()
    from_line[here] = pairs[low]

    line_all().wait_recv()

    sums = []
    for n in range(2):
        parts = [from_line[8 * n + q] for q in range(8)]
        while len(parts) > 1:
            parts = [a + b for a, b in zip(parts[::2], parts[1::2])]
        sums.append(parts[0])
    jac = jnp.concatenate(
        [
            sums[0][:, : 2 * BLOCK],
            sums[1][:, :BLOCK] + sums[0][:, 2 * BLOCK :],
            sums[1][:, BLOCK : 2 * BLOCK],
        ],
        axis=1,
    )
    value = jac
    for n in range(hops):
        lagged = pltpu.roll(value, length - 2**n, 1)
        value = value + powers[n] * jnp.where(ids < length - 2**n, lagged, 0.0)
    wide[0] = jac
    wide[1] = value
    lanes = pl.ds(pl.multiple_of(horizon * BLOCK, BLOCK), BLOCK)
    jac_out[...] = wide[0, :, lanes]
    value_out[...] = wide[1, :, lanes]
    plane_all().wait_send()
    line_all().wait_send()


def local(expect, steady_dist, policy_deriv, lottery_index, type_trans, migration, discount):
    types, assets = lottery_index.shape
    cols, states = policy_deriv.shape
    count = expect.shape[0]
    far = pl.BlockSpec(memory_space=pltpu.HBM)
    vmem = pl.BlockSpec(memory_space=pltpu.VMEM)
    return pl.pallas_call(
        flow_kernel,
        out_shape=[jax.ShapeDtypeStruct((2, count), f32)] * 2,
        in_specs=[far] * 7,
        out_specs=[vmem, vmem],
        scratch_shapes=[
            pltpu.VMEM((2, count, states), bf),
            pltpu.VMEM((ONE_HOP + 1, types * cols, assets), bf),
            pltpu.VMEM((2, cols, 2 * count), f32),
            pltpu.VMEM((4 * cols, 3 * BLOCK), f32),
            pltpu.VMEM((4, 2, 3 * BLOCK), f32),
            pltpu.VMEM((15, 8, 3 * BLOCK), f32),
            pltpu.VMEM((16, 2, 3 * BLOCK), f32),
            pltpu.VMEM((4, 1, count), f32),
            pltpu.VMEM((2, 2, 4 * BLOCK), f32),
            pltpu.VMEM((9, 2, 4 * BLOCK), f32),
            pltpu.VMEM((cols, states), bf),
            pltpu.VMEM((cols, states), bf),
            pltpu.VMEM((states // BLOCK, BLOCK), f32),
            pltpu.VMEM((types, assets), jnp.int32),
            pltpu.VMEM((2, types, assets), jnp.int16),
            pltpu.VMEM((types, types), f32),
            pltpu.VMEM((2, types), bf),
            pltpu.VMEM((3, 8, BLOCK), f32),
            pltpu.VMEM((3, types, BLOCK), f32),
            pltpu.VMEM((assets // BLOCK, types, BLOCK), f32),
            pltpu.VMEM((4, types, BLOCK), f32),
            pltpu.VMEM((2 * types * 16, types * 16), bf),
            pltpu.VMEM((2, types, 32 * assets // BLOCK, 2 * BLOCK), bf),
            pltpu.VMEM((2, 2, types * 16, assets), bf),
            pltpu.VMEM((1, count), f32),
            pltpu.SemaphoreType.DMA((6 + PARTS,)),
            pltpu.SemaphoreType.DMA((STEPS + 1,)),
            pltpu.SemaphoreType.DMA((STEPS + 1, CHUNKS)),
            pltpu.SemaphoreType.DMA((types,)),
            pltpu.SemaphoreType.DMA((48 + PARTS,)),
            pltpu.SemaphoreType.DMA((48 + PARTS,)),
        ],
        compiler_params=pltpu.CompilerParams(
            collective_id=0, has_side_effects=True, vmem_limit_bytes=52 * 2**20
        ),
        name="flow",
    )(
        *[
            pltpu.with_memory_space_constraint(value, pltpu.HBM)
            for value in (
                expect,
                policy_deriv,
                steady_dist.reshape(-1, BLOCK),
                lottery_index,
                type_trans,
                migration.reshape(2, types),
                discount.reshape(1, count),
            )
        ]
    )


def solution(mesh):
    return jax.shard_map(
        local,
        mesh=mesh,
        in_specs=(
            P("horizon", "state"),
            P("state"),
            P("horizon", "state"),
            P("state", None),
            P(),
            P("state", None, None),
            P("horizon"),
        ),
        out_specs=(P("state", "horizon"), P("state", "horizon")),
        check_vma=False,
    )
```

time: 1220 us -> 165 us (0.14)
  waiting for transfers between devices: 1070 us -> 0 us
  Pallas kernels: 0 us -> 163 us
  matrix products: 60.2 us -> 0 us
  starting transfers between devices: 31.1 us -> 0 us
  local copies, waits for them, and re-layouts: 23.8 us -> 1.13 us
  between operations: 15.7 us -> 0.64 us
    psum x1 -> x0, waiting for transfers between devices: 599 us -> none  [local(): flow_total = lax.psum(flow_part, 'state')]
    ppermute x5 -> x0, waiting for transfers between devices: 357 us -> none  [the longest x4 357 us: shifted(): return lax.ppermute(block, axis, route)]
    pallas_call x0 -> x1, Pallas kernels: none -> 163 us  [local(): pl.pallas_call(flow_kernel, out_shape=[jax.ShapeDtypeStruct((2, count), f...]
    all_gather x1 -> x0, waiting for transfers between devices: 118 us -> none  [local(): all_shift = lax.all_gather(own_shift, 'horizon', axis=0, tiled=True)]
    dot_general x7 -> x0, matrix products: 60.2 us -> none  [the longest x3 23.2 us: against(): lax.dot_general(left_rows, right_rows, (((1,), (1,)), ((), ())), preferre...]
    ppermute x5 -> x0, starting transfers between devices: 31 us -> none  [the longest x1 23.6 us: shifted_2(): return lax.ppermute(value, axis, pairs)]
  transfers between devices with their start and end apart: 7 -> 0, of which waited for: 4 -> 0; matrix products, arithmetic and copies ran while one was open for 2% -> 0% of each run, Pallas kernels for 0% -> 0%
where the time goes in v1:
time: 165 us
  Pallas kernels  163 us (99%)
    pallas_call x1, Pallas kernels, local(): pl.pallas_call(flow_kernel, out_shape=[jax.ShapeDtypeStruct((2, count), f...  163 us

profile of v1, /device:TPU:1, one launch (start us, length us, event | category | flops | bytes accessed | tf_op | source)
XLA Modules:
  0.0 164.9 jit_solution(14425556370533270720)
XLA Ops:
  0.6 163.1 %flow.1 = (f32[2,128]{1,0:T(2,128)S(1)}, f32[2,128]{1,0:T(2,128)S(1)}) custom-call(bf16[128,32768]{1,0:T(8,128)(2,1)} %expect_in.1, bf16[32,32768]{1,0:T(8,128)(2,1)} %policy_in.1, f32[256,128]{1,0:T(8,128)} %bitcast.3, s32[16,2048]{1,0:T(8,128)} %index_in.1, f32[16,16]{1,0:T(8,128)} %trans_in.1, bf16[2,16]{1,0:T(2,128)(2,1)} %bitcast.4, f32[1,128]{1,0:T(1,128)} %bitcast.5), custom_call_target="tpu_custom_call" | custom-call | tf_op jit(solution)/shard_map/flow/pallas_call | solution.py:502
  163.8 0.6 copy.11
  164.3 0.6 copy.12

commit v2 on v1

--- a/solution.py
+++ b/solution.py
@@ -106,7 +106,7 @@
 
 
 def flow_kernel(
-    expect_in, policy_in, steady_in, index_in, trans_in, migration_in, discount_in, jac_out, value_out,
+    expect_in, policy_in, steady_in, index_in, trans_in, migration_in, discount_in, out,
     lines, held, flow, half, pairs, from_plane, from_line, betas, wide, powers,
     mass, raw, steady, nodes, short, trans, moves, rates, weights, offsets, keys, kron, moved, landed, discount,
     local_sem, send_sem, recv_sem, last_sem, tail_send, tail_recv,
@@ -487,8 +487,7 @@
     wide[0] = jac
     wide[1] = value
     lanes = pl.ds(pl.multiple_of(horizon * BLOCK, BLOCK), BLOCK)
-    jac_out[...] = wide[0, :, lanes]
-    value_out[...] = wide[1, :, lanes]
+    out[...] = wide[:, :, lanes]
     plane_all().wait_send()
     line_all().wait_send()
 
@@ -499,11 +498,11 @@
     count = expect.shape[0]
     far = pl.BlockSpec(memory_space=pltpu.HBM)
     vmem = pl.BlockSpec(memory_space=pltpu.VMEM)
-    return pl.pallas_call(
+    both = pl.pallas_call(
         flow_kernel,
-        out_shape=[jax.ShapeDtypeStruct((2, count), f32)] * 2,
+        out_shape=jax.ShapeDtypeStruct((2, 2, count), f32),
         in_specs=[far] * 7,
-        out_specs=[vmem, vmem],
+        out_specs=vmem,
         scratch_shapes=[
             pltpu.VMEM((2, count, states), bf),
             pltpu.VMEM((ONE_HOP + 1, types * cols, assets), bf),
@@ -555,6 +554,7 @@
             )
         ]
     )
+    return both[0], both[1]
 
 
 def solution(mesh):

time: 165 us -> 164 us (level)
  no operation moved by 1% of the time
where the time goes in v2:
time: 164 us
  Pallas kernels  163 us (99%)
    pallas_call x1, Pallas kernels, local(): pl.pallas_call(flow_kernel, out_shape=jax.ShapeDtypeStruct((2, 2, count),...  163 us

profile of v2, /device:TPU:1, one launch (start us, length us, event | category | flops | bytes accessed | tf_op | source)
XLA Modules:
  0.0 164.3 jit_solution(8820238642495428489)
XLA Ops:
  0.6 163.1 %flow.1 = f32[2,2,128]{2,1,0:T(2,128)S(1)} custom-call(bf16[128,32768]{1,0:T(8,128)(2,1)} %expect_in.1, bf16[32,32768]{1,0:T(8,128)(2,1)} %policy_in.1, f32[256,128]{1,0:T(8,128)} %bitcast.7, s32[16,2048]{1,0:T(8,128)} %index_in.1, f32[16,16]{1,0:T(8,128)} %trans_in.1, bf16[2,16]{1,0:T(2,128)(2,1)} %bitcast.8, f32[1,128]{1,0:T(1,128)} %bitcast.9), custom_call_target="tpu_custom_call" | custom-call | tf_op jit(solution)/shard_map/flow/pallas_call | solution.py:501
  163.8 0.6 slice_bitcast_fusion
